TPU v7x, 256 devices: a whole 4x4x8 slice. The times are simulated.
256 devices in a mesh: dp: 4 (over y), pipe: 4 (over z_hi), tensor: 16 (over x, z_lo, core).
Axes of the slice: x: 4, y: 4, z: 8 (z_hi: 4, z_lo: 2; z = z_hi * 2 + z_lo), core: 2. Of those that a mesh axis runs over, the one named last changes fastest.
Arguments:
- hidden: bfloat16 [4, 2048, 14336], P('pipe', 'dp', 'tensor'), parts along dimension 1, may hold values from -6 to 6
- residual: bfloat16 [4, 2048, 4096], P('pipe', ('dp', 'tensor')), parts along dimension 1, may hold values from -6 to 6
- norm_gain: float32 [4, 4096], P('pipe'), may hold values from 0.5 to 1.5
- down_weight: bfloat16 [4, 14336, 4096], P('pipe', 'tensor'), may hold values from -0.046875 to 0.046875
- qkv_weight: bfloat16 [4, 4096, 6144], P('pipe', None, 'tensor'), may hold values from -0.09375 to 0.09375
Outputs:
- section_output: bfloat16 [4, 2048, 4096], P('pipe', ('dp', 'tensor')), parts along dimension 1
- projections: bfloat16 [4, 2048, 6144], P('pipe', 'dp', 'tensor'), parts along dimension 1
There are 4 independent parts, one for each index of `dp`. A program takes and returns all parts, laid end to end along the dimension named above; an argument that names none is the same for every part. Nothing has to cross between parts.
All inputs are finite; a program needn't handle non-finite values.
Results may differ from a plain program's by a relative error of at most 0.022.
Values may be sent and summed in bfloat16 or wider, within the bound.
No kernel may reach another device: no remote copies, remote signals or barrier semaphores. Data moves between devices by JAX's collectives and lax.ppermute only.
A program may use at most 64 MiB of HBM per device.

v0:
```python
import jax
import jax.numpy as jnp
from jax import lax
from jax.sharding import PartitionSpec as P


def passed_along(value, axis, steps):
    count = lax.axis_size(axis)
    pairs = [(source, (source + steps) % count) for source in range(count)]
    return lax.ppermute(value, axis, pairs)


def normalize(values, gain_row):
    wide = values.astype(jnp.float32)
    scaler = lax.rsqrt(jnp.mean(wide * wide, axis=-1, keepdims=True) + 1e-05)
    return (wide * scaler * gain_row).astype(jnp.bfloat16)


def shards(hidden, residual, norm_gain, down_weight, qkv_weight):
    hidden_rows = hidden[0]
    resid_rows = residual[0]
    gain_row = norm_gain[0]
    down_local = down_weight[0]
    qkv_local = qkv_weight[0]
    tok_rows = resid_rows.shape[0]
    resid_full = lax.all_gather(resid_rows, "tensor", axis=0, tiled=True)
    summed = lax.psum(
        jnp.dot(hidden_rows, down_local, preferred_element_type=jnp.float32).astype(jnp.bfloat16),
        "tensor",
    ).astype(jnp.float32)
    full_rows = (resid_full.astype(jnp.float32) + summed).astype(jnp.bfloat16)
    offset = lax.axis_index("tensor") * tok_rows
    section_output = lax.dynamic_slice_in_dim(full_rows, offset, tok_rows, 0)
    arrived = passed_along(full_rows, "pipe", 1)
    normed = normalize(arrived, gain_row)
    projections = jnp.dot(normed, qkv_local, preferred_element_type=jnp.float32).astype(
        jnp.bfloat16
    )
    return (section_output[None], projections[None])


def solution(mesh):
    return jax.shard_map(
        shards,
        mesh=mesh,
        in_specs=(
            P("pipe", "dp", "tensor"),
            P("pipe", ("dp", "tensor"), None),
            P("pipe", None),
            P("pipe", "tensor", None),
            P("pipe", None, "tensor"),
        ),
        out_specs=(P("pipe", ("dp", "tensor"), None), P("pipe", "dp", "tensor")),
        check_vma=False,
    )
```

profile of v0, /device:TPU:2, one launch (start us, length us, event | category | flops | bytes accessed | tf_op | source)
XLA Modules:
  0.0 410.3 jit_solution(18110407928350033155)
XLA Ops:
  7.2 0.0 copy-start
  7.2 0.0 all-reduce.2.cloned.1.call-start
  7.2 10.0 %fusion.6 = bf16[512,4096]{1,0:T(8,128)(2,1)} fusion(bf16[1,896,4096]{2,1,0:T(8,128)(2,1)} %param.8, bf16[1,512,896]{2,1,0:T(8,128)(2,1)} %param.5), kind=kOutput, calls=%fused_computation.9 | convolution fusion | flops 3760193536 | bytes 12451840 | tf_op jit(solution)/shard_map/dot_general | solution.py:28
  17.2 0.0 all-reduce.2.cloned.1.call-update
  17.2 0.0 all-gather.3.cloned.1.call-start
  17.3 0.7 all-gather.3.cloned.1.call-update
  18.0 137.3 %all-reduce.2.cloned.1.call-done = bf16[512,4096]{1,0:T(8,128)(2,1)} async-done(((bf16[512,4096]{1,0:T(8,128)(2,1)}), bf16[512,4096]{1,0:T(8,128)(2,1)}) %all-reduce.2.cloned.1.call-update) | async-done | bytes 4194320 | tf_op jit(solution)/shard_map/psum | solution.py:27
  155.2 46.2 %all-gather.3.cloned.1.call-done = bf16[1,512,4096]{2,1,0:T(8,128)(2,1)} async-done(((bf16[1,32,4096]{2,1,0:T(8,128)(2,1)}), bf16[1,512,4096]{2,1,0:T(8,128)(2,1)}) %all-gather.3.cloned.1.call-update) | async-done | bytes 4194320 | tf_op jit(solution)/shard_map/all_gather | solution.py:26
  201.5 7.2 %fusion.3 = bf16[512,4096]{1,0:T(8,128)(2,1)} fusion(bf16[512,4096]{1,0:T(8,128)(2,1)} %all-reduce.2.cloned.1.call-done, bf16[1,512,4096]{2,1,0:T(8,128)(2,1)} %all-gather.3.cloned.1.call-done), kind=kLoop, calls=%fused_computation.6 | loop fusion | flops 8388608 | bytes 12582912 | tf_op jit(solution)/shard_map/convert_element_type | solution.py:31
  208.6 0.0 copy-start.1
  208.6 2.6 collective-permute-start
  211.2 1.7 dynamic-slice_bitcast_fusion
  212.9 182.2 %collective-permute-done = bf16[512,4096]{1,0:T(8,128)(2,1)} collective-permute-done((bf16[512,4096]{1,0:T(8,128)(2,1)}, bf16[512,4096]{1,0:T(8,128)(2,1)}, u32[]{:S(2)}, u32[]{:S(2)}) %collective-permute-start) | collective-permute-done | bytes 4194336 | tf_op jit(solution)/shard_map/ppermute | solution.py:10
  395.1 3.1 fusion
  398.1 0.0 copy-done
  398.2 0.0 copy-done.1
  398.2 5.3 %fusion.19 = bf16[1,512,384]{2,1,0:T(8,128)(2,1)} fusion(bf16[1,4096,384]{2,1,0:T(8,128)(2,1)S(1)} %copy-done, bf16[512,4096]{1,0:T(8,128)(2,1)} %collective-permute-done, f32[4096]{0:T(1024)S(1)} %bitcast.23, f32[512]{0:T(512)S(1)} %add_rsqrt_fusion), kind=kOutput, calls=%fused_computation.15 | convolution fusion | flops 1619197952 | bytes 7751680 | tf_op jit(solution)/shard_map/dot_general | solution.py:36
  (1 shorter events, 0.0 us)
Async XLA Ops:
  7.2 391.0 %copy-start = (bf16[1,4096,384]{2,1,0:T(8,128)(2,1)S(1)}, bf16[1,4096,384]{2,1,0:T(8,128)(2,1)}, u32[]{:S(2)}) copy-start(bf16[1,4096,384]{2,1,0:T(8,128)(2,1)} %param.9) | copy-start | bytes 9437188
  7.2 148.1 %all-reduce.2.cloned.1.call-start = ((), (), s32[]{:S(2)}) async-start(), calls=%async_computation | async-start | bytes 8388608 | tf_op jit(solution)/shard_map/psum | solution.py:27
  17.2 184.2 %all-gather.3.cloned.1.call-start = ((), (), s32[]{:S(2)}) async-start(), calls=%async_computation.1 | async-start | bytes 4456448 | tf_op jit(solution)/shard_map/all_gather | solution.py:26
  208.6 189.5 %copy-start.1 = (f32[1,4096]{1,0:T(1,128)S(1)}, f32[1,4096]{1,0:T(1,128)}, u32[]{:S(2)}) copy-start(f32[1,4096]{1,0:T(1,128)} %param.7) | copy-start | bytes 49156
  208.6 186.4 %collective-permute-start = (bf16[512,4096]{1,0:T(8,128)(2,1)}, bf16[512,4096]{1,0:T(8,128)(2,1)}, u32[]{:S(2)}, u32[]{:S(2)}) collective-permute-start(bf16[512,4096]{1,0:T(8,128)(2,1)} %fusion.3), channel_id=1, source_target_pairs={{0,16},{16,32},{32,48},{48,0},{1,17},{17,33},{33,49},{49,1},{2,18}... | collective-permute-start | bytes 12582920 | tf_op jit(solution)/shard_map/ppermute | solution.py:10
Sparse Core Ops, SparseCore 0:
  17.3 137.8 all-reduce.1
  157.1 44.3 all-gather.2
where the time goes:
time: 410 us
  waiting for transfers between devices  366 us (89%)
  matrix products  15.3 us (4%)
  between operations  14.1 us (3%)
  other arithmetic  10.3 us (3%)
    ppermute x1, waiting for transfers between devices, passed_along(): return lax.ppermute(value, axis, pairs)  182 us
    psum x1, waiting for transfers between devices, shards(): lax.psum(jnp.dot(hidden_rows, down_local, preferred_element_type=jnp.floa...  137 us
    all_gather x1, waiting for transfers between devices, shards(): resid_full = lax.all_gather(resid_rows, 'tensor', axis=0, tiled=True)  46.2 us
    dot_general x1, matrix products, shards(): jnp.dot(hidden_rows, down_local, preferred_element_type=jnp.float32)  9.96 us
  transfers between devices with their start and end apart: 3, of which 3 were waited for; matrix products, arithmetic and copies ran while one was open for 0% of the time, Pallas kernels for 0%

commit v1 on v0

--- a/solution.py
+++ b/solution.py
@@ -23,7 +23,16 @@
     down_local = down_weight[0]
     qkv_local = qkv_weight[0]
     tok_rows = resid_rows.shape[0]
-    resid_full = lax.all_gather(resid_rows, "tensor", axis=0, tiled=True)
+    _lay_samples_all = lambda field: jnp.concatenate(
+        lax.all_to_all(
+            jnp.stack([field for _ in range(lax.axis_size("tensor"))], axis=0),
+            axis_name="tensor",
+            split_axis=0,
+            concat_axis=0,
+        ),
+        axis=0,
+    )
+    resid_full = _lay_samples_all(resid_rows)
     summed = lax.psum(
         jnp.dot(hidden_rows, down_local, preferred_element_type=jnp.float32).astype(jnp.bfloat16),
         "tensor",

time: 410 us -> 390 us (0.951)
  waiting for transfers between devices: 366 us -> 333 us
  starting transfers between devices: 2.64 us -> 9.13 us
    all_gather x1 -> x0, waiting for transfers between devices: 46.2 us -> none  [shards(): resid_full = lax.all_gather(resid_rows, 'tensor', axis=0, tiled=True)]
    psum x1, waiting for transfers between devices: 137 us -> 153 us  [shards(): lax.psum(jnp.dot(hidden_rows, down_local, preferred_element_type=jnp.floa...]
    all_to_all x0 -> x1, starting transfers between devices: none -> 6.55 us  [shards(): lax.all_to_all(jnp.stack([field for _ in range(lax.axis_size('tensor'))],...]
  transfers between devices with their start and end apart: 3 -> 3, of which waited for: 3 -> 2; matrix products, arithmetic and copies ran while one was open for 0% -> 3% of each run, Pallas kernels for 0% -> 0%
where the time goes in v1:
time: 390 us; the launch traced here: 387 us
  waiting for transfers between devices  333 us (85%)
  matrix products  15.1 us (4%)
  between operations  14.1 us (4%)
  other arithmetic  10.3 us (3%)
  starting transfers between devices  9.13 us (2%)
  local copies, waits for them, and re-layouts  5.28 us (1%)
    ppermute x1, waiting for transfers between devices, passed_along(): return lax.ppermute(value, axis, pairs)  180 us
    psum x1, waiting for transfers between devices, shards(): lax.psum(jnp.dot(hidden_rows, down_local, preferred_element_type=jnp.floa...  153 us
    dot_general x1, matrix products, shards(): jnp.dot(hidden_rows, down_local, preferred_element_type=jnp.float32)  9.83 us
  transfers between devices with their start and end apart: 3, of which 2 were waited for; matrix products, arithmetic and copies ran while one was open for 3% of the time, Pallas kernels for 0%

profile of v1, /device:TPU:2, one launch (start us, length us, event | category | flops | bytes accessed | tf_op | source)
XLA Modules:
  0.0 386.6 jit_solution(16743926435729313868)
XLA Ops:
  7.2 0.0 copy-start
  7.2 3.6 stack.3
  10.7 6.5 %all-to-all-start = ((bf16[16,32,4096]{2,1,0:T(8,128)(2,1)}), bf16[16,32,4096]{2,1,0:T(8,128)(2,1)}, u32[]{:S(2)}, u32[]{:S(2)}) async-start(bf16[16,32,4096]{2,1,0:T(8,128)(2,1)} %stack.3), calls=%async_computation | async-start | bytes 8388608 | tf_op jit(solution)/shard_map/all_to_all | solution.py:27
  17.3 0.0 all-reduce.2.cloned.1.call-start
  17.3 9.8 %fusion.6 = bf16[512,4096]{1,0:T(8,128)(2,1)} fusion(bf16[1,896,4096]{2,1,0:T(8,128)(2,1)} %param.8, bf16[1,512,896]{2,1,0:T(8,128)(2,1)} %param.5), kind=kOutput, calls=%fused_computation.9 | convolution fusion | flops 3760193536 | bytes 12451840 | tf_op jit(solution)/shard_map/dot_general | solution.py:37
  27.2 0.0 all-reduce.2.cloned.1.call-update
  27.2 153.1 %all-reduce.2.cloned.1.call-done = bf16[512,4096]{1,0:T(8,128)(2,1)} async-done(((bf16[512,4096]{1,0:T(8,128)(2,1)}), bf16[512,4096]{1,0:T(8,128)(2,1)}) %all-reduce.2.cloned.1.call-update) | async-done | bytes 4194320 | tf_op jit(solution)/shard_map/psum | solution.py:36
  180.3 0.0 all-to-all-done
  180.3 7.2 %fusion.3 = bf16[512,4096]{1,0:T(8,128)(2,1)} fusion(bf16[512,4096]{1,0:T(8,128)(2,1)} %all-reduce.2.cloned.1.call-done, bf16[16,32,4096]{2,1,0:T(8,128)(2,1)} %all-to-all-done), kind=kLoop, calls=%fused_computation.6 | loop fusion | flops 8388608 | bytes 12582912 | tf_op jit(solution)/shard_map/convert_element_type | solution.py:40
  187.5 0.0 copy-start.1
  187.5 2.5 collective-permute-start
  190.0 1.7 dynamic-slice_bitcast_fusion
  191.7 179.6 %collective-permute-done = bf16[512,4096]{1,0:T(8,128)(2,1)} collective-permute-done((bf16[512,4096]{1,0:T(8,128)(2,1)}, bf16[512,4096]{1,0:T(8,128)(2,1)}, u32[]{:S(2)}, u32[]{:S(2)}) %collective-permute-start) | collective-permute-done | bytes 4194336 | tf_op jit(solution)/shard_map/ppermute | solution.py:10
  371.3 3.1 fusion
  374.4 0.0 copy-done
  374.4 0.0 copy-done.1
  374.5 5.3 %fusion.19 = bf16[1,512,384]{2,1,0:T(8,128)(2,1)} fusion(bf16[1,4096,384]{2,1,0:T(8,128)(2,1)S(1)} %copy-done, bf16[512,4096]{1,0:T(8,128)(2,1)} %collective-permute-done, f32[4096]{0:T(1024)S(1)} %bitcast.25, f32[512]{0:T(512)S(1)} %add_rsqrt_fusion), kind=kOutput, calls=%fused_computation.15 | convolution fusion | flops 1619197952 | bytes 7751680 | tf_op jit(solution)/shard_map/dot_general | solution.py:45
  (1 shorter events, 0.0 us)
Async XLA Ops:
  7.2 367.3 %copy-start = (bf16[1,4096,384]{2,1,0:T(8,128)(2,1)S(1)}, bf16[1,4096,384]{2,1,0:T(8,128)(2,1)}, u32[]{:S(2)}) copy-start(bf16[1,4096,384]{2,1,0:T(8,128)(2,1)} %param.9) | copy-start | bytes 9437188
  10.7 169.5 %all-to-all-start = ((bf16[16,32,4096]{2,1,0:T(8,128)(2,1)}), bf16[16,32,4096]{2,1,0:T(8,128)(2,1)}, u32[]{:S(2)}, u32[]{:S(2)}) async-start(bf16[16,32,4096]{2,1,0:T(8,128)(2,1)} %stack.3), calls=%async_computation | async-start | bytes 8388608 | tf_op jit(solution)/shard_map/all_to_all | solution.py:27
  17.3 163.0 %all-reduce.2.cloned.1.call-start = ((), (), s32[]{:S(2)}) async-start(), calls=%async_computation.1 | async-start | bytes 8388608 | tf_op jit(solution)/shard_map/psum | solution.py:36
  187.5 187.0 %copy-start.1 = (f32[1,4096]{1,0:T(1,128)S(1)}, f32[1,4096]{1,0:T(1,128)}, u32[]{:S(2)}) copy-start(f32[1,4096]{1,0:T(1,128)} %param.7) | copy-start | bytes 49156
  187.5 183.9 %collective-permute-start = (bf16[512,4096]{1,0:T(8,128)(2,1)}, bf16[512,4096]{1,0:T(8,128)(2,1)}, u32[]{:S(2)}, u32[]{:S(2)}) collective-permute-start(bf16[512,4096]{1,0:T(8,128)(2,1)} %fusion.3), channel_id=1, source_target_pairs={{0,16},{16,32},{32,48},{48,0},{1,17},{17,33},{33,49},{49,1},{2,18}... | collective-permute-start | bytes 12582920 | tf_op jit(solution)/shard_map/ppermute | solution.py:10
Sparse Core Ops, SparseCore 0:
  27.3 152.9 all-reduce.1
